TPU v7x, 512 devices: a whole 4x8x8 slice. The times are simulated.
512 devices in a mesh: req: 128 (over y, z, core), tp: 4 (over x).
Axes of the slice: x: 4, y: 8, z: 8, core: 2. Of those that a mesh axis runs over, the one named last changes fastest.
Arguments:
- attn_out: bfloat16 [8192, 2048], P('req', 'tp'), may hold values from -6 to 6
- w_out: bfloat16 [2048, 2048], P('tp'), may hold values from -0.125 to 0.125
- residual: bfloat16 [8192, 2048], P('req', 'tp'), may hold values from -6 to 6
- routes: int32 [8192, 6], P('req'), may hold values from 0 to 127, all different within a row; in each aligned block of 64 rows (0 to 63, 64 to 127, ...) at most 6 rows name the same one
- gates: float32 [8192, 6], P('req'), may hold values from 0.05 to 1
- w_gate: bfloat16 [128, 2048, 1024], P('req', None, 'tp'), as said below
- w_up: bfloat16 [128, 2048, 1024], P('req', None, 'tp'), as said below
- w_down: bfloat16 [128, 1024, 2048], P('req', None, 'tp'), as said below
- norm_gain: float32 [2048], P('tp'), may hold values from 0.1 to 1.9
Outputs:
- normed: bfloat16 [8192, 2048], P('req', 'tp')
Inputs may be any that keep to these rules, and one draw needn't show every extreme that they name: `routes`: each row names 6 different slots. In the 64 rows of one index of req no slot is named by more than 6 rows, a bound that some block reaches. `w_gate`: slots 2 e and 2 e + 1 hold the same expert e: their weights are equal. `w_up`: slots 2 e and 2 e + 1 hold the same expert e: their weights are equal. `w_down`: slots 2 e and 2 e + 1 hold the same expert e: their weights are equal.
All inputs are finite; a program needn't handle non-finite values.
Results may differ from a plain program's by a relative error of at most 0.0056.
Values may be sent and summed in bfloat16 or wider, within the bound.
A program may use at most 64 MiB of HBM per device.

v0:
```python
import jax
import jax.numpy as jnp
from jax import lax
from jax.sharding import PartitionSpec as P


def body(attn_out, w_out, residual, routes, gates, w_gate, w_up, w_down, norm_gain):
    row_count = attn_out.shape[0]
    part_width = residual.shape[1]
    full_width = w_out.shape[1]
    route_count = routes.shape[1]
    slot_count = lax.axis_size("req")
    capacity = max(2, min(row_count, 2 * row_count * route_count // slot_count))
    tp_index = lax.axis_index("tp")
    partial_value = jnp.dot(attn_out, w_out, preferred_element_type=jnp.float32)
    own_block = lax.dynamic_slice_in_dim(partial_value, tp_index * part_width, part_width, 1)
    partial_value = lax.dynamic_update_slice_in_dim(
        partial_value, own_block + residual.astype(jnp.float32), tp_index * part_width, 1
    )
    flat_routes = routes.reshape(-1)
    one_hot = (flat_routes[:, None] == jnp.arange(slot_count, dtype=jnp.int32)[None, :]).astype(
        jnp.int32
    )
    position = jnp.sum(one_hot * (jnp.cumsum(one_hot, axis=0) - 1), axis=1)
    dest_index = flat_routes * capacity + position
    row_ids = jnp.repeat(jnp.arange(row_count, dtype=jnp.int32), route_count)
    source_row = jnp.zeros((slot_count * capacity,), jnp.int32).at[dest_index].set(row_ids)
    gate_local = w_gate[0]
    up_local = w_up[0]
    down_local = w_down[0]
    projected = lax.psum(partial_value, "tp")
    own_part = lax.dynamic_slice_in_dim(projected, tp_index * part_width, part_width, 1)
    outgoing = projected.astype(jnp.bfloat16)[source_row].reshape(slot_count, capacity, full_width)
    incoming = lax.all_to_all(outgoing, "req", split_axis=0, concat_axis=0, tiled=True)
    expert_rows = incoming.reshape(slot_count * capacity, full_width)
    gate_act = jnp.dot(expert_rows, gate_local, preferred_element_type=jnp.float32)
    up_act = jnp.dot(expert_rows, up_local, preferred_element_type=jnp.float32)
    hidden = (jax.nn.silu(gate_act) * up_act).astype(jnp.bfloat16)
    expert_out = jnp.dot(
        lax.all_gather(hidden, "tp", axis=1, tiled=True),
        down_local,
        preferred_element_type=jnp.float32,
    )
    expert_out = expert_out.astype(jnp.bfloat16).reshape(slot_count, capacity, down_local.shape[1])
    returned = lax.all_to_all(expert_out, "req", split_axis=0, concat_axis=0, tiled=True)
    picked = returned.reshape(slot_count * capacity, part_width)[dest_index]
    picked = picked.reshape(row_count, route_count, part_width).astype(jnp.float32)
    routed_sum = jnp.sum(picked * gates[:, :, None], axis=1)
    combined = own_part + routed_sum
    square_part = jnp.sum(combined * combined, axis=1)
    square_total = lax.psum(square_part, "tp")
    scale = lax.rsqrt(square_total / full_width + 1e-06)
    return (combined * scale[:, None] * norm_gain[None, :]).astype(jnp.bfloat16)


def solution(mesh):
    placed = (
        P("req", "tp"),
        P("tp", None),
        P("req", "tp"),
        P("req", None),
        P("req", None),
        P("req", None, "tp"),
        P("req", None, "tp"),
        P("req", None, "tp"),
        P("tp"),
    )
    return jax.shard_map(
        body, mesh=mesh, in_specs=placed, out_specs=P("req", "tp"), check_vma=False
    )
```

profile of v0, /device:TPU:8, one launch (start us, length us, event | category | flops | bytes accessed | tf_op | source)
XLA Modules:
  0.0 315.9 jit_solution(1539475655118343820)
XLA Ops:
  6.5 0.0 copy-start
  6.5 0.0 all-reduce.2.cloned.1.call-start
  6.5 1.6 copy-done
  8.1 1.3 fusion.12
  9.4 0.9 add_dynamic-update-slice_fusion
  10.3 0.0 copy-start.2
  10.3 0.8 copy-done.2
  11.1 0.0 all-reduce.2.cloned.1.call-update
  11.1 0.0 all-gather.2.cloned.1.call-start
  11.2 0.0 copy-done.3
  11.2 0.1 copy.12
  11.3 0.1 eq.29
  11.4 0.1 eq.25
  11.6 0.1 copy.14
  11.7 0.2 fusion.5
  12.0 0.1 add_add_fusion
  12.0 0.1 copy.11
  12.1 0.1 mul.61
  12.3 0.1 reshape.96
  12.4 0.2 fusion.7
  12.7 2.9 scatter_custom_fusion
  15.6 53.9 %all-reduce.2.cloned.1.call-done = f32[64,2048]{1,0:T(8,128)} async-done(((f32[64,2048]{1,0:T(8,128)}), f32[64,2048]{1,0:T(8,128)}) %all-reduce.2.cloned.1.call-update) | async-done | bytes 524304 | tf_op jit(solution)/shard_map/psum | solution.py:31
  69.5 1.1 convert_element_type.27
  70.6 4.3 %gather_fusion = bf16[768,2048]{1,0:T(8,128)(2,1)} fusion(bf16[64,2048]{1,0:T(8,128)(2,1)S(1)} %convert_element_type.27, s32[1024]{0:T(1024)S(1)} %pad_clamp_fusion.1), kind=kCustom, calls=%fused_computation | custom fusion | bytes 6294528 | tf_op jit(solution)/shard_map/gather | solution.py:33
  74.9 6.3 %reshape.71 = bf16[128,6,2048]{2,1,0:T(8,128)(2,1)} reshape(bf16[768,2048]{1,0:T(8,128)(2,1)} %gather_fusion) | data formatting | bytes 6291456 | tf_op jit(solution)/shard_map/reshape | solution.py:33
  81.1 111.0 %all_to_all.10 = bf16[128,6,2048]{2,1,0:T(8,128)(2,1)} all-to-all(bf16[128,6,2048]{2,1,0:T(8,128)(2,1)} %reshape.71), channel_id=1, replica_groups=mesh['req'=128,'tp'=4] {'req'}, dimensions={0} | all-to-all | bytes 6291456 | tf_op jit(solution)/shard_map/all_to_all | solution.py:34
  192.1 6.3 %reshape.72 = bf16[768,2048]{1,0:T(8,128)(2,1)} reshape(bf16[128,6,2048]{2,1,0:T(8,128)(2,1)} %all_to_all.10) | data formatting | bytes 6291456 | tf_op jit(solution)/shard_map/reshape | solution.py:35
  198.4 3.3 %fusion.3 = f32[768,256]{1,0:T(8,128)S(1)} fusion(bf16[768,2048]{1,0:T(8,128)(2,1)} %reshape.72, bf16[1,2048,256]{2,1,0:T(8,128)(2,1)} %param.14), kind=kOutput, calls=%fused_computation.8 | convolution fusion | flops 805306368 | bytes 4980736 | tf_op jit(solution)/shard_map/dot_general | solution.py:36
  201.7 0.0 copy-done.1
  201.8 0.1 copy-done.6
  201.9 1.7 fusion
  203.6 0.0 all-gather.2.cloned.1.call-update
  203.6 38.7 %all-gather.2.cloned.1.call-done = bf16[768,1024]{1,0:T(8,128)(2,1)} async-done(((bf16[768,256]{1,0:T(8,128)(2,1)}), bf16[768,1024]{1,0:T(8,128)(2,1)}) %all-gather.2.cloned.1.call-update) | async-done | bytes 1572880 | tf_op jit(solution)/shard_map/all_gather | solution.py:40
  242.3 2.7 convolution_convert_fusion
  245.0 0.0 copy-start.4
  245.0 1.3 reshape.73
  246.3 14.6 %all-to-all-start.1 = ((bf16[128,6,512]{2,1,0:T(8,128)(2,1)}), bf16[128,6,512]{2,1,0:T(8,128)(2,1)}, u32[]{:S(2)}, u32[]{:S(2)}) async-start(bf16[128,6,512]{2,1,0:T(8,128)(2,1)} %reshape.73), calls=%async_computation.1 | async-start | bytes 2097152 | tf_op jit(solution)/shard_map/all_to_all | solution.py:45
  260.9 0.0 copy-done.4
  260.9 0.7 copy.16
  261.6 30.2 %all-to-all-done.1 = bf16[128,6,512]{2,1,0:T(8,128)(2,1)} async-done(((bf16[128,6,512]{2,1,0:T(8,128)(2,1)}), bf16[128,6,512]{2,1,0:T(8,128)(2,1)}, u32[]{:S(2)}, u32[]{:S(2)}) %all-to-all-start.1) | async-done | bytes 786464 | tf_op jit(solution)/shard_map/all_to_all | solution.py:45
  291.9 1.4 reshape.74
  293.2 0.0 copy-start.5
  293.3 2.1 gather_fusion.1
  295.3 0.1 reshape.75
  295.4 1.1 multiply_reduce_fusion
  296.6 1.0 multiply_reduce_fusion.1
  297.6 9.8 %psum.15 = f32[64]{0:T(128)S(1)} all-reduce(f32[64]{0:T(128)S(1)} %multiply_reduce_fusion.1), channel_id=1, replica_groups=mesh['req'=128,'tp'=4] {'tp'}, use_global_device_ids=true, to_apply=%region_7.8 | all-reduce | flops 64 | bytes 512 | tf_op jit(solution)/shard_map/psum | solution.py:51
  307.4 1.6 multiply_convert_fusion
  (14 shorter events, 0.1 us)
Async XLA Ops:
  6.5 1.6 copy-start
  6.5 4.6 %copy-start.3 = (s32[64,6]{0,1:T(8,128)S(1)}, s32[64,6]{0,1:T(8,128)}, u32[]{:S(2)}) copy-start(s32[64,6]{0,1:T(8,128)} %param.12) | copy-start | bytes 4612
  6.5 63.0 %all-reduce.2.cloned.1.call-start = ((), (), s32[]{:S(2)}) async-start(), calls=%async_computation.2 | async-start | bytes 1048576 | tf_op jit(solution)/shard_map/psum | solution.py:31
  10.3 0.8 copy-start.2
  11.1 231.1 %all-gather.2.cloned.1.call-start = ((), (), s32[]{:S(2)}) async-start(), calls=%async_computation.3 | async-start | bytes 1966080 | tf_op jit(solution)/shard_map/all_gather | solution.py:40
  198.4 3.3 %copy-start.1 = (bf16[768,2048]{1,0:T(8,128)(2,1)S(1)}, bf16[768,2048]{1,0:T(8,128)(2,1)}, u32[]{:S(2)}) copy-start(bf16[768,2048]{1,0:T(8,128)(2,1)} %reshape.72) | copy-start | bytes 9437188
  198.4 3.4 %copy-start.6 = (bf16[1,2048,256]{2,1,0:T(8,128)(2,1)S(1)}, bf16[1,2048,256]{2,1,0:T(8,128)(2,1)}, u32[]{:S(2)}) copy-start(bf16[1,2048,256]{2,1,0:T(8,128)(2,1)} %param.15) | copy-start | bytes 3145732
  245.0 15.9 %copy-start.4 = (f32[64,6]{0,1:T(8,128)S(1)}, f32[64,6]{0,1:T(8,128)}, u32[]{:S(2)}) copy-start(f32[64,6]{0,1:T(8,128)} %param.13) | copy-start | bytes 4612
  246.3 45.6 %all-to-all-start.1 = ((bf16[128,6,512]{2,1,0:T(8,128)(2,1)}), bf16[128,6,512]{2,1,0:T(8,128)(2,1)}, u32[]{:S(2)}, u32[]{:S(2)}) async-start(bf16[128,6,512]{2,1,0:T(8,128)(2,1)} %reshape.73), calls=%async_computation.1 | async-start | bytes 2097152 | tf_op jit(solution)/shard_map/all_to_all | solution.py:45
  293.2 14.2 %copy-start.5 = (f32[512]{0:T(512)S(1)}, f32[512]{0:T(512)}, u32[]{:S(2)}) copy-start(f32[512]{0:T(512)} %param.17) | copy-start | bytes 6148
Sparse Core Ops, SparseCore 0:
  11.3 58.2 all-reduce.1
  203.7 38.5 all-gather.1
where the time goes:
time: 317 us; the launch traced here: 316 us
  waiting for transfers between devices  123 us (39%)
  blocking collectives  121 us (38%)
  local copies, waits for them, and re-layouts  28.7 us (9%)
  starting transfers between devices  14.7 us (5%)
  between operations  13.6 us (4%)
  matrix products  9.02 us (3%)
  other arithmetic  6.31 us (2%)
    all_to_all x1, blocking collectives, body(): lax.all_to_all(outgoing, 'req', split_axis=0, concat_axis=0, tiled=True)  111 us
    psum x1, waiting for transfers between devices, body(): projected = lax.psum(partial_value, 'tp')  53.9 us
    all_gather x1, waiting for transfers between devices, body(): lax.all_gather(hidden, 'tp', axis=1, tiled=True)  38.7 us
    all_to_all x1, waiting for transfers between devices, body(): lax.all_to_all(expert_out, 'req', split_axis=0, concat_axis=0, tiled=True)  30.2 us
    all_to_all x1, starting transfers between devices, body(): lax.all_to_all(expert_out, 'req', split_axis=0, concat_axis=0, tiled=True)  14.6 us
    psum x1, blocking collectives, body(): square_total = lax.psum(square_part, 'tp')  9.8 us
  transfers between devices with their start and end apart: 3, of which 3 were waited for; matrix products, arithmetic and copies ran while one was open for 2% of the time, Pallas kernels for 0%

commit v1 on v0

--- a/solution.py
+++ b/solution.py
@@ -2,6 +2,22 @@
 import jax.numpy as jnp
 from jax import lax
 from jax.sharding import PartitionSpec as P
+
+
+def ring_gather(x, axis, dim):
+    ways, here, step = (lax.axis_size(axis), lax.axis_index(axis), x.shape[dim])
+    shape = [n * ways if d == dim else n for d, n in enumerate(x.shape)]
+    full = lax.dynamic_update_slice_in_dim(jnp.zeros(shape, x.dtype), x, here * step, axis=dim)
+    going_up = going_down = x
+    for far in range(1, ways // 2 + 1):
+        going_up = lax.ppermute(going_up, axis, [(d, (d + 1) % ways) for d in range(ways)])
+        full = lax.dynamic_update_slice_in_dim(full, going_up, (here - far) % ways * step, axis=dim)
+        if 2 * far < ways:
+            going_down = lax.ppermute(going_down, axis, [(d, (d - 1) % ways) for d in range(ways)])
+            full = lax.dynamic_update_slice_in_dim(
+                full, going_down, (here + far) % ways * step, axis=dim
+            )
+    return full
 
 
 def body(attn_out, w_out, residual, routes, gates, w_gate, w_up, w_down, norm_gain):
@@ -37,9 +53,7 @@
     up_act = jnp.dot(expert_rows, up_local, preferred_element_type=jnp.float32)
     hidden = (jax.nn.silu(gate_act) * up_act).astype(jnp.bfloat16)
     expert_out = jnp.dot(
-        lax.all_gather(hidden, "tp", axis=1, tiled=True),
-        down_local,
-        preferred_element_type=jnp.float32,
+        ring_gather(hidden, "tp", 1), down_local, preferred_element_type=jnp.float32
     )
     expert_out = expert_out.astype(jnp.bfloat16).reshape(slot_count, capacity, down_local.shape[1])
     returned = lax.all_to_all(expert_out, "req", split_axis=0, concat_axis=0, tiled=True)

time: 317 us -> 307 us (0.968)
  the two profiles are of different devices: /device:TPU:8 before, /device:TPU:10 now
where the time goes in v1:
time: 307 us; the launch traced here: 306 us
  waiting for transfers between devices  192 us (63%)
  starting transfers between devices  43.5 us (14%)
  local copies, waits for them, and re-layouts  32.4 us (11%)
  between operations  13.7 us (4%)
  blocking collectives  10.7 us (3%)
  matrix products  8.47 us (3%)
  other arithmetic  5.47 us (2%)
    all_to_all x1, waiting for transfers between devices, body(): lax.all_to_all(outgoing, 'req', split_axis=0, concat_axis=0, tiled=True)  96.3 us
    psum x1, waiting for transfers between devices, body(): projected = lax.psum(partial_value, 'tp')  53 us
    all_to_all x1, waiting for transfers between devices, body(): lax.all_to_all(expert_out, 'req', split_axis=0, concat_axis=0, tiled=True)  30.2 us
    all_to_all x1, starting transfers between devices, body(): lax.all_to_all(expert_out, 'req', split_axis=0, concat_axis=0, tiled=True)  19.3 us
    all_to_all x1, starting transfers between devices, body(): lax.all_to_all(outgoing, 'req', split_axis=0, concat_axis=0, tiled=True)  14.6 us
    ppermute x2, waiting for transfers between devices, ring_gather(): lax.ppermute(going_up, axis, [(d, (d + 1) % ways) for d in range(ways)])  12.3 us
    psum x1, blocking collectives, body(): square_total = lax.psum(square_part, 'tp')  10.7 us
    ppermute x2, starting transfers between devices, ring_gather(): lax.ppermute(going_up, axis, [(d, (d + 1) % ways) for d in range(ways)])  7.41 us
  transfers between devices with their start and end apart: 6, of which 5 were waited for; matrix products, arithmetic and copies ran while one was open for 2% of the time, Pallas kernels for 0%

profile of v1, /device:TPU:10, one launch (start us, length us, event | category | flops | bytes accessed | tf_op | source)
XLA Modules:
  0.0 306.1 jit_solution(10488028393315566425)
XLA Ops:
  6.6 1.6 copy-done
  8.1 1.3 fusion.12
  9.5 0.8 copy-done.2
  10.3 0.0 all-reduce.2.cloned.1.call-update
  10.3 0.1 copy.12
  10.4 0.1 eq.33
  10.6 0.1 eq.29
  10.7 0.1 copy.14
  10.8 0.2 fusion.5
  11.1 0.1 add_add_fusion
  11.2 0.1 copy.11
  11.3 0.1 mul.73
  11.4 0.1 reshape.96
  11.6 0.2 fusion.7
  11.8 2.9 scatter_custom_fusion
  14.8 53.0 %all-reduce.2.cloned.1.call-done = f32[64,2048]{1,0:T(8,128)} async-done(((f32[64,2048]{1,0:T(8,128)}), f32[64,2048]{1,0:T(8,128)}) %all-reduce.2.cloned.1.call-update) | async-done | bytes 524304 | tf_op jit(solution)/shard_map/psum | solution.py:47
  67.7 1.1 convert_element_type.27
  68.8 4.3 %gather_fusion = bf16[768,2048]{1,0:T(8,128)(2,1)} fusion(bf16[64,2048]{1,0:T(8,128)(2,1)S(1)} %convert_element_type.27, s32[1024]{0:T(1024)S(1)} %pad_clamp_fusion.1), kind=kCustom, calls=%fused_computation | custom fusion | bytes 6294528 | tf_op jit(solution)/shard_map/gather | solution.py:49
  73.1 6.3 %reshape.71 = bf16[128,6,2048]{2,1,0:T(8,128)(2,1)} reshape(bf16[768,2048]{1,0:T(8,128)(2,1)} %gather_fusion) | data formatting | bytes 6291456 | tf_op jit(solution)/shard_map/reshape | solution.py:49
  79.3 14.6 %all-to-all-start = ((bf16[128,6,2048]{2,1,0:T(8,128)(2,1)}), bf16[128,6,2048]{2,1,0:T(8,128)(2,1)}, u32[]{:S(2)}, u32[]{:S(2)}) async-start(bf16[128,6,2048]{2,1,0:T(8,128)(2,1)} %reshape.71), calls=%async_computation | async-start | bytes 8388608 | tf_op jit(solution)/shard_map/all_to_all | solution.py:50
  94.0 96.3 %all-to-all-done = bf16[128,6,2048]{2,1,0:T(8,128)(2,1)} async-done(((bf16[128,6,2048]{2,1,0:T(8,128)(2,1)}), bf16[128,6,2048]{2,1,0:T(8,128)(2,1)}, u32[]{:S(2)}, u32[]{:S(2)}) %all-to-all-start) | async-done | bytes 3145760 | tf_op jit(solution)/shard_map/all_to_all | solution.py:50
  190.3 6.3 %reshape.72 = bf16[768,2048]{1,0:T(8,128)(2,1)} reshape(bf16[128,6,2048]{2,1,0:T(8,128)(2,1)} %all-to-all-done) | data formatting | bytes 6291456 | tf_op jit(solution)/shard_map/reshape | solution.py:51
  196.6 3.0 fusion.3
  199.7 0.2 broadcast_in_dim.6
  199.9 1.7 constant_dynamic-update-slice_fusion.2
  201.6 1.2 copy-done.3
  202.8 3.7 %collective-permute-start = (bf16[768,256]{1,0:T(8,128)(2,1)}, bf16[768,256]{1,0:T(8,128)(2,1)S(1)}, u32[]{:S(2)}, u32[]{:S(2)}) collective-permute-start(bf16[768,256]{1,0:T(8,128)(2,1)} %get-tuple-element.6), channel_id=1, source_target_pairs={{0,1},{1,2},{2,3},{3,0},{4,5},{5,6},{6,7},{7,4},{8,9},{9,10},{10,1... | collective-permute-start | bytes 1179656 | tf_op jit(solution)/shard_map/ppermute | solution.py:13
  206.5 2.1 collective-permute-start.1
  208.6 6.0 %collective-permute-done = bf16[768,256]{1,0:T(8,128)(2,1)S(1)} collective-permute-done((bf16[768,256]{1,0:T(8,128)(2,1)}, bf16[768,256]{1,0:T(8,128)(2,1)S(1)}, u32[]{:S(2)}, u32[]{:S(2)}) %collective-permute-start) | collective-permute-done | bytes 393248 | tf_op jit(solution)/shard_map/ppermute | solution.py:13
  214.7 3.7 %collective-permute-start.2 = (bf16[768,256]{1,0:T(8,128)(2,1)S(1)}, bf16[768,256]{1,0:T(8,128)(2,1)S(1)}, u32[]{:S(2)}, u32[]{:S(2)}) collective-permute-start(bf16[768,256]{1,0:T(8,128)(2,1)S(1)} %collective-permute-done), channel_id=1, source_target_pairs={{0,1},{1,2},{2,3},{3,0},{4,5},{5,6},{6,7},{7,4},{8,9},{9,10},{10,1... | collective-permute-start | bytes 1179656 | tf_op jit(solution)/shard_map/ppermute | solution.py:13
  218.4 0.0 copy-start.10
  218.4 0.8 constant_dynamic-update-slice_fusion.1
  219.3 0.8 constant_dynamic-update-slice_fusion
  220.1 6.3 %collective-permute-done.2 = bf16[768,256]{1,0:T(8,128)(2,1)S(1)} collective-permute-done((bf16[768,256]{1,0:T(8,128)(2,1)S(1)}, bf16[768,256]{1,0:T(8,128)(2,1)S(1)}, u32[]{:S(2)}, u32[]{:S(2)}) %collective-permute-start.2) | collective-permute-done | bytes 393248 | tf_op jit(solution)/shard_map/ppermute | solution.py:13
  226.4 0.8 constant_dynamic-update-slice_fusion.3
  227.2 2.4 convolution_convert_fusion
  229.6 1.3 reshape.73
  230.9 19.3 %all-to-all-start.1 = ((bf16[128,6,512]{2,1,0:T(8,128)(2,1)}), bf16[128,6,512]{2,1,0:T(8,128)(2,1)}, u32[]{:S(2)}, u32[]{:S(2)}) async-start(bf16[128,6,512]{2,1,0:T(8,128)(2,1)} %reshape.73), calls=%async_computation.1 | async-start | bytes 2097152 | tf_op jit(solution)/shard_map/all_to_all | solution.py:59
  250.2 0.7 copy.16
  250.9 30.2 %all-to-all-done.1 = bf16[128,6,512]{2,1,0:T(8,128)(2,1)} async-done(((bf16[128,6,512]{2,1,0:T(8,128)(2,1)}), bf16[128,6,512]{2,1,0:T(8,128)(2,1)}, u32[]{:S(2)}, u32[]{:S(2)}) %all-to-all-start.1) | async-done | bytes 786464 | tf_op jit(solution)/shard_map/all_to_all | solution.py:59
  281.1 1.4 reshape.74
  282.5 2.1 gather_fusion.1
  284.6 0.0 copy-start.7
  284.6 0.1 reshape.75
  284.7 1.1 multiply_reduce_fusion
  285.9 1.0 multiply_reduce_fusion.1
  286.9 10.7 %psum.15 = f32[64]{0:T(128)S(1)} all-reduce(f32[64]{0:T(128)S(1)} %multiply_reduce_fusion.1), channel_id=1, replica_groups=mesh['req'=128,'tp'=4] {'tp'}, use_global_device_ids=true, to_apply=%region_7.8 | all-reduce | flops 64 | bytes 512 | tf_op jit(solution)/shard_map/psum | solution.py:65
  297.6 1.6 multiply_convert_fusion
  (30 shorter events, 0.2 us)
Async XLA Ops:
  6.5 1.6 copy-start
  6.5 2.9 copy-start.4
  6.5 3.8 %copy-start.5 = (s32[64,6]{0,1:T(8,128)S(1)}, s32[64,6]{0,1:T(8,128)}, u32[]{:S(2)}) copy-start(s32[64,6]{0,1:T(8,128)} %param.12) | copy-start | bytes 4612
  6.5 61.2 %all-reduce.2.cloned.1.call-start = ((), (), s32[]{:S(2)}) async-start(), calls=%async_computation.2 | async-start | bytes 1048576 | tf_op jit(solution)/shard_map/psum | solution.py:47
  9.5 0.8 copy-start.2
  79.3 111.0 %all-to-all-start = ((bf16[128,6,2048]{2,1,0:T(8,128)(2,1)}), bf16[128,6,2048]{2,1,0:T(8,128)(2,1)}, u32[]{:S(2)}, u32[]{:S(2)}) async-start(bf16[128,6,2048]{2,1,0:T(8,128)(2,1)} %reshape.71), calls=%async_computation | async-start | bytes 8388608 | tf_op jit(solution)/shard_map/all_to_all | solution.py:50
  94.0 102.7 %copy-start.8 = (bf16[1,2048,256]{2,1,0:T(8,128)(2,1)S(1)}, bf16[1,2048,256]{2,1,0:T(8,128)(2,1)}, u32[]{:S(2)}) copy-start(bf16[1,2048,256]{2,1,0:T(8,128)(2,1)} %param.14) | copy-start | bytes 3145732
  196.6 3.2 %copy-start.1 = (bf16[768,2048]{1,0:T(8,128)(2,1)S(1)}, bf16[768,2048]{1,0:T(8,128)(2,1)}, u32[]{:S(2)}) copy-start(bf16[768,2048]{1,0:T(8,128)(2,1)} %reshape.72) | copy-start | bytes 9437188
  196.6 3.2 %copy-start.9 = (bf16[1,2048,256]{2,1,0:T(8,128)(2,1)S(1)}, bf16[1,2048,256]{2,1,0:T(8,128)(2,1)}, u32[]{:S(2)}) copy-start(bf16[1,2048,256]{2,1,0:T(8,128)(2,1)} %param.15) | copy-start | bytes 3145732
  201.6 1.2 copy-start.3
  202.8 11.9 %collective-permute-start = (bf16[768,256]{1,0:T(8,128)(2,1)}, bf16[768,256]{1,0:T(8,128)(2,1)S(1)}, u32[]{:S(2)}, u32[]{:S(2)}) collective-permute-start(bf16[768,256]{1,0:T(8,128)(2,1)} %get-tuple-element.6), channel_id=1, source_target_pairs={{0,1},{1,2},{2,3},{3,0},{4,5},{5,6},{6,7},{7,4},{8,9},{9,10},{10,1... | collective-permute-start | bytes 1179656 | tf_op jit(solution)/shard_map/ppermute | solution.py:13
  206.5 12.8 %collective-permute-start.1 = (bf16[768,256]{1,0:T(8,128)(2,1)}, bf16[768,256]{1,0:T(8,128)(2,1)S(1)}, u32[]{:S(2)}, u32[]{:S(2)}) collective-permute-start(bf16[768,256]{1,0:T(8,128)(2,1)} %get-tuple-element.6), channel_id=1, source_target_pairs={{0,3},{1,0},{2,1},{3,2},{4,7},{5,4},{6,5},{7,6},{8,11},{9,8},{10,9... | collective-permute-start | bytes 1179656 | tf_op jit(solution)/shard_map/ppermute | solution.py:16
  214.7 11.7 %collective-permute-start.2 = (bf16[768,256]{1,0:T(8,128)(2,1)S(1)}, bf16[768,256]{1,0:T(8,128)(2,1)S(1)}, u32[]{:S(2)}, u32[]{:S(2)}) collective-permute-start(bf16[768,256]{1,0:T(8,128)(2,1)S(1)} %collective-permute-done), channel_id=1, source_target_pairs={{0,1},{1,2},{2,3},{3,0},{4,5},{5,6},{6,7},{7,4},{8,9},{9,10},{10,1... | collective-permute-start | bytes 1179656 | tf_op jit(solution)/shard_map/ppermute | solution.py:13
  218.4 8.7 %copy-start.10 = (bf16[1,1024,512]{2,1,0:T(8,128)(2,1)S(1)}, bf16[1,1024,512]{2,1,0:T(8,128)(2,1)}, u32[]{:S(2)}) copy-start(bf16[1,1024,512]{2,1,0:T(8,128)(2,1)} %param.16) | copy-start | bytes 3145732
  229.6 20.6 %copy-start.6 = (f32[64,6]{0,1:T(8,128)S(1)}, f32[64,6]{0,1:T(8,128)}, u32[]{:S(2)}) copy-start(f32[64,6]{0,1:T(8,128)} %param.13) | copy-start | bytes 4612
  230.9 50.3 %all-to-all-start.1 = ((bf16[128,6,512]{2,1,0:T(8,128)(2,1)}), bf16[128,6,512]{2,1,0:T(8,128)(2,1)}, u32[]{:S(2)}, u32[]{:S(2)}) async-start(bf16[128,6,512]{2,1,0:T(8,128)(2,1)} %reshape.73), calls=%async_computation.1 | async-start | bytes 2097152 | tf_op jit(solution)/shard_map/all_to_all | solution.py:59
  284.6 13.0 %copy-start.7 = (f32[512]{0:T(512)S(1)}, f32[512]{0:T(512)}, u32[]{:S(2)}) copy-start(f32[512]{0:T(512)} %param.17) | copy-start | bytes 6148
Sparse Core Ops, SparseCore 0:
  10.4 57.2 all-reduce.1
